TPU v7x, 128 devices: a whole 4x4x4 slice. The times are simulated.
128 devices in a mesh: seq: 32 (over z, x_lo, y), fsdp: 4 (over x_hi, core).
Axes of the slice: x: 4 (x_hi: 2, x_lo: 2; x = x_hi * 2 + x_lo), y: 4, z: 4, core: 2. Of those that a mesh axis runs over, the one named last changes fastest.
Arguments:
- inputs: bfloat16 [4, 16384, 640], P('fsdp', 'seq'), may hold values from -6 to 6
- doc_start: int32 [4, 16384], P('fsdp', 'seq'), may hold values from 0 to 15360, as said below
- w_query: bfloat16 [640, 1024], P('fsdp'), may hold values from -0.25 to 0.25
- w_key: bfloat16 [640, 256], P('fsdp'), may hold values from -0.25 to 0.25
- w_value: bfloat16 [640, 256], P('fsdp'), may hold values from -0.25 to 0.25
- w_output: bfloat16 [1024, 640], P('fsdp'), may hold values from -0.375 to 0.375
- w_gate: bfloat16 [640, 2048], P('fsdp'), may hold values from -0.25 to 0.25
- w_up: bfloat16 [640, 2048], P('fsdp'), may hold values from -0.25 to 0.25
- w_down: bfloat16 [2048, 640], P('fsdp'), may hold values from -0.125 to 0.125
- norm_attn_in: bfloat16 [640], P('fsdp'), may hold values from 0.099609375 to 1.8984375
- norm_attn_out: bfloat16 [640], P('fsdp'), may hold values from 0.099609375 to 1.8984375
- norm_ffn_in: bfloat16 [640], P('fsdp'), may hold values from 0.099609375 to 1.8984375
- norm_ffn_out: bfloat16 [640], P('fsdp'), may hold values from 0.099609375 to 1.8984375
- norm_query: bfloat16 [256], P('fsdp'), may hold values from 0.099609375 to 1.8984375
- norm_key: bfloat16 [256], P('fsdp'), may hold values from 0.099609375 to 1.8984375
- cotangent: bfloat16 [4, 16384, 640], P('fsdp', 'seq'), may hold values from -6 to 6
Outputs:
- layer_out: bfloat16 [4, 16384, 640], P('fsdp', 'seq')
- input_grad: float32 [4, 16384, 640], P('fsdp', 'seq')
- query_grad: float32 [640, 1024], P('fsdp')
- key_grad: float32 [640, 256], P('fsdp')
- value_grad: float32 [640, 256], P('fsdp')
- output_grad: float32 [1024, 640], P('fsdp')
- gate_grad: float32 [640, 2048], P('fsdp')
- up_grad: float32 [640, 2048], P('fsdp')
- down_grad: float32 [2048, 640], P('fsdp')
- attn_in_grad: float32 [640], P('fsdp')
- attn_out_grad: float32 [640], P('fsdp')
- ffn_in_grad: float32 [640], P('fsdp')
- ffn_out_grad: float32 [640], P('fsdp')
- query_norm_grad: float32 [256], P('fsdp')
- key_norm_grad: float32 [256], P('fsdp')
Inputs may be any that keep to these rules, and one draw needn't show every extreme that they name: Each row of 16384 tokens holds exactly two documents, each of 1024 tokens or more: doc_start is 0 up to the second document's first index and that index from there on; in some row the second document is exactly 1024 tokens long.
All inputs are finite; a program needn't handle non-finite values.
Results may differ from a plain program's by a relative error of at most 0.034.
Values may be sent and summed in bfloat16 or wider, within the bound.
A program may use at most 192 MiB of HBM per device.

v0:
```python
import jax
import jax.numpy as jnp
from jax import lax
from jax.sharding import PartitionSpec as P

WINDOW = 512
epsilon = 1e-06
rope_base = 10000.0
masked_value = -1e30


def side_by_side(arrays, axis, dim, along):
    ends, at = ([], 0)
    for a in arrays[:-1]:
        at += a.shape[along]
        ends.append(at)
    both = jnp.concatenate(arrays, axis=along)
    return tuple(jnp.split(lax.all_gather(both, axis, axis=dim, tiled=True), ends, axis=along))


def from_behind(shard, axis, by):
    count = lax.axis_size(axis)
    pairs = [(i, i + by) for i in range(count) if 0 <= i + by < count]
    return lax.ppermute(shard, axis, pairs)


def side_by_side_2(arrays, axis, dim, along):
    both = jnp.concatenate(arrays, axis=along)
    out, at, gathered = (lax.psum_scatter(both, axis, scatter_dimension=dim, tiled=True), 0, [])
    for a in arrays:
        gathered.append(lax.slice_in_dim(out, at, at + a.shape[along], axis=along))
        at += a.shape[along]
    return tuple(gathered)


def rms_scale(values, gains):
    return values * lax.rsqrt(jnp.mean(values * values, -1, keepdims=True) + epsilon) * gains


def rope_tables(positions, head_width):
    half_width = head_width // 2
    frequency = rope_base ** (-(jnp.arange(half_width, dtype=jnp.float32) * (2.0 / head_width)))
    angles = positions[:, None] * frequency[None, :]
    cosine = jnp.cos(angles)
    sine_part = jnp.sin(angles)
    return (jnp.concatenate([cosine, cosine], -1), jnp.concatenate([sine_part, sine_part], -1))


def rotate(values, cosine, sine_part):
    half_width = values.shape[-1] // 2
    turned = jnp.concatenate([-values[..., half_width:], values[..., :half_width]], -1)
    return values * cosine + turned * sine_part


def forward_dot(left, right):
    return jnp.dot(left, right, preferred_element_type=jnp.float32)


def contract_rows(left, right):
    return lax.dot_general(
        left, right, (((0,), (0,)), ((), ())), preferred_element_type=jnp.float32
    )


def contract_cols(left, right):
    return lax.dot_general(
        left, right, (((1,), (1,)), ((), ())), preferred_element_type=jnp.float32
    )


def gated_product(gate_value, up_value):
    return jax.nn.gelu(gate_value, approximate=True) * up_value


def body(
    inputs,
    doc_start,
    w_query,
    w_key,
    w_value,
    w_output,
    w_gate,
    w_up,
    w_down,
    norm_attn_in,
    norm_attn_out,
    norm_ffn_in,
    norm_ffn_out,
    norm_query,
    norm_key,
    cotangent,
):
    gathered = (
        *side_by_side((w_query, w_key, w_value), "fsdp", 0, 1),
        lax.all_gather(w_output, "fsdp", axis=0, tiled=True),
        *side_by_side((w_gate, w_up), "fsdp", 0, 1),
        lax.all_gather(w_down, "fsdp", axis=0, tiled=True),
        lax.all_gather(norm_attn_in, "fsdp", axis=0, tiled=True),
        lax.all_gather(norm_attn_out, "fsdp", axis=0, tiled=True),
        lax.all_gather(norm_ffn_in, "fsdp", axis=0, tiled=True),
        lax.all_gather(norm_ffn_out, "fsdp", axis=0, tiled=True),
        lax.all_gather(norm_query, "fsdp", axis=0, tiled=True),
        lax.all_gather(norm_key, "fsdp", axis=0, tiled=True),
    )
    full_query, full_key, full_value, full_output, full_gate, full_up, full_down = gathered[:7]
    gain_attn_in, gain_attn_out, gain_ffn_in, gain_ffn_out, gain_query, gain_key = [
        member.astype(jnp.float32) for member in gathered[7:]
    ]
    length = inputs.shape[1]
    head_width = full_key.shape[1]
    head_count = full_query.shape[1] // head_width
    span_count = -(-(WINDOW - 1) // length)
    block_index = lax.axis_index("seq")
    row_index = block_index * length + jnp.arange(length, dtype=jnp.int32)
    doc_local = doc_start[0]
    positions = (row_index - doc_local).astype(jnp.float32)
    cosine, sine_part = rope_tables(positions, head_width)
    source = inputs[0].astype(jnp.float32)
    normed, pull_attn_in = jax.vjp(rms_scale, source, gain_attn_in)
    normed_low = normed.astype(jnp.bfloat16)
    query_raw = forward_dot(normed_low, full_query)
    key_raw = forward_dot(normed_low, full_key)
    value_raw = forward_dot(normed_low, full_value)

    def shape_query(raw_rows, gains):
        return rotate(
            rms_scale(raw_rows.reshape(length, head_count, head_width), gains),
            cosine[:, None, :],
            sine_part[:, None, :],
        )

    def shape_key(raw_rows, gains):
        return rotate(rms_scale(raw_rows, gains), cosine, sine_part)

    query_rows, pull_query = jax.vjp(shape_query, query_raw, gain_query)
    key_rows, pull_key = jax.vjp(shape_key, key_raw, gain_key)
    query_low = query_rows.astype(jnp.bfloat16)
    key_low = key_rows.astype(jnp.bfloat16)
    value_low = value_raw.astype(jnp.bfloat16)
    distance = 1
    key_from, value_from = from_behind((key_low, value_low), "seq", distance)
    earlier_keys = [key_from]
    earlier_values = [value_from]
    all_keys = jnp.concatenate(earlier_keys + [key_low], 0)
    all_values = jnp.concatenate(earlier_values + [value_low], 0)
    key_index = (block_index - span_count) * length + jnp.arange(
        (span_count + 1) * length, dtype=jnp.int32
    )
    visible = (
        (key_index[None, :] >= doc_local[:, None])
        & (key_index[None, :] <= row_index[:, None])
        & (row_index[:, None] - key_index[None, :] < WINDOW)
    )
    score_scale = head_width ** (-0.5)

    def score_rows():
        raw_scores = (
            jnp.einsum("thd,kd->htk", query_low, all_keys, preferred_element_type=jnp.float32)
            * score_scale
        )
        return jnp.where(visible[None], raw_scores, masked_value)

    scores = score_rows()
    row_max = jnp.max(scores, -1, keepdims=True)
    shifted = jnp.exp(scores - row_max)
    row_total = jnp.sum(shifted, -1, keepdims=True)
    soft_weights = shifted / row_total
    log_total = row_max + jnp.log(row_total)
    weights_low = soft_weights.astype(jnp.bfloat16)
    attended = jnp.einsum(
        "htk,kd->thd", weights_low, all_values, preferred_element_type=jnp.float32
    )
    attended = attended.reshape(length, head_count * head_width).astype(jnp.bfloat16)
    projected = forward_dot(attended, full_output)
    branch_one, pull_attn_out = jax.vjp(rms_scale, projected, gain_attn_out)
    hidden_one = source + branch_one
    normed_two, pull_ffn_in = jax.vjp(rms_scale, hidden_one, gain_ffn_in)
    normed_two_low = normed_two.astype(jnp.bfloat16)
    gate_value = forward_dot(normed_two_low, full_gate)
    up_value = forward_dot(normed_two_low, full_up)
    product, pull_product = jax.vjp(gated_product, gate_value, up_value)
    product_low = product.astype(jnp.bfloat16)
    down_value = forward_dot(product_low, full_down)
    branch_two, pull_ffn_out = jax.vjp(rms_scale, down_value, gain_ffn_out)
    layer_out = (hidden_one + branch_two).astype(jnp.bfloat16)[None]
    again = (
        *side_by_side((w_query, w_key, w_value), "fsdp", 0, 1),
        lax.all_gather(w_output, "fsdp", axis=0, tiled=True),
        *side_by_side((w_gate, w_up), "fsdp", 0, 1),
        lax.all_gather(w_down, "fsdp", axis=0, tiled=True),
    )
    back_query, back_key, back_value, back_output, back_gate, back_up, back_down = again
    upstream = cotangent[0].astype(jnp.float32)
    d_down, grad_ffn_out = pull_ffn_out(upstream)
    d_down_low = d_down.astype(jnp.bfloat16)
    grad_down = contract_rows(product_low, d_down_low)
    d_product = contract_cols(d_down_low, back_down)
    d_gate, d_up = pull_product(d_product)
    d_gate_low = d_gate.astype(jnp.bfloat16)
    d_up_low = d_up.astype(jnp.bfloat16)
    grad_gate = contract_rows(normed_two_low, d_gate_low)
    grad_up = contract_rows(normed_two_low, d_up_low)
    d_normed_two = contract_cols(d_gate_low, back_gate) + contract_cols(d_up_low, back_up)
    d_hidden_part, grad_ffn_in = pull_ffn_in(d_normed_two)
    d_hidden = upstream + d_hidden_part
    d_projected, grad_attn_out = pull_attn_out(d_hidden)
    d_projected_low = d_projected.astype(jnp.bfloat16)
    grad_output = contract_rows(attended, d_projected_low)
    d_attended = (
        contract_cols(d_projected_low, back_output)
        .astype(jnp.bfloat16)
        .reshape(length, head_count, head_width)
    )
    soft_again = jnp.exp(score_rows() - log_total)
    d_soft = jnp.einsum("thd,kd->htk", d_attended, all_values, preferred_element_type=jnp.float32)
    inner_sum = jnp.sum(soft_again * d_soft, -1, keepdims=True)
    d_scores = (soft_again * (d_soft - inner_sum)).astype(jnp.bfloat16)
    d_queries = (
        jnp.einsum("htk,kd->thd", d_scores, all_keys, preferred_element_type=jnp.float32)
        * score_scale
    )
    d_keys = (
        jnp.einsum("htk,thd->kd", d_scores, query_low, preferred_element_type=jnp.float32)
        * score_scale
    )
    d_values = jnp.einsum(
        "htk,thd->kd",
        soft_again.astype(jnp.bfloat16),
        d_attended,
        preferred_element_type=jnp.float32,
    )
    d_key_own = d_keys[span_count * length :]
    d_value_own = d_values[span_count * length :]
    distance = 1
    first_row = (span_count - distance) * length
    key_back = from_behind(
        d_keys[first_row : first_row + length].astype(jnp.bfloat16), "seq", -distance
    ).astype(jnp.float32)
    value_back = from_behind(
        d_values[first_row : first_row + length].astype(jnp.bfloat16), "seq", -distance
    ).astype(jnp.float32)
    d_key_own = d_key_own + key_back
    d_value_own = d_value_own + value_back
    d_key_raw, grad_key_norm = pull_key(d_key_own)
    d_query_raw, grad_query_norm = pull_query(d_queries)
    d_query_low = d_query_raw.astype(jnp.bfloat16)
    d_key_low = d_key_raw.astype(jnp.bfloat16)
    d_value_low = d_value_own.astype(jnp.bfloat16)
    grad_query = contract_rows(normed_low, d_query_low)
    grad_key = contract_rows(normed_low, d_key_low)
    grad_value = contract_rows(normed_low, d_value_low)
    d_normed = (
        contract_cols(d_query_low, back_query)
        + contract_cols(d_key_low, back_key)
        + contract_cols(d_value_low, back_value)
    )
    d_source, grad_attn_in = pull_attn_in(d_normed)
    input_grad = (d_hidden + d_source)[None]
    shares = (
        *tuple(
            (
                part.astype(jnp.float32)
                for part in side_by_side_2(
                    (
                        grad_query.astype(jnp.bfloat16),
                        grad_key.astype(jnp.bfloat16),
                        grad_value.astype(jnp.bfloat16),
                    ),
                    "fsdp",
                    0,
                    1,
                )
            )
        ),
        lax.psum_scatter(
            grad_output.astype(jnp.bfloat16), "fsdp", scatter_dimension=0, tiled=True
        ).astype(jnp.float32),
        *tuple(
            (
                part.astype(jnp.float32)
                for part in side_by_side_2(
                    (grad_gate.astype(jnp.bfloat16), grad_up.astype(jnp.bfloat16)), "fsdp", 0, 1
                )
            )
        ),
        lax.psum_scatter(
            grad_down.astype(jnp.bfloat16), "fsdp", scatter_dimension=0, tiled=True
        ).astype(jnp.float32),
        lax.psum_scatter(
            grad_attn_in.astype(jnp.bfloat16), "fsdp", scatter_dimension=0, tiled=True
        ).astype(jnp.float32),
        lax.psum_scatter(
            grad_attn_out.astype(jnp.bfloat16), "fsdp", scatter_dimension=0, tiled=True
        ).astype(jnp.float32),
        lax.psum_scatter(
            grad_ffn_in.astype(jnp.bfloat16), "fsdp", scatter_dimension=0, tiled=True
        ).astype(jnp.float32),
        lax.psum_scatter(
            grad_ffn_out.astype(jnp.bfloat16), "fsdp", scatter_dimension=0, tiled=True
        ).astype(jnp.float32),
        lax.psum_scatter(
            grad_query_norm.astype(jnp.bfloat16), "fsdp", scatter_dimension=0, tiled=True
        ).astype(jnp.float32),
        lax.psum_scatter(
            grad_key_norm.astype(jnp.bfloat16), "fsdp", scatter_dimension=0, tiled=True
        ).astype(jnp.float32),
    )
    finals = (
        lax.psum(shares[0].astype(jnp.bfloat16), "seq").astype(jnp.float32),
        lax.psum(shares[1].astype(jnp.bfloat16), "seq").astype(jnp.float32),
        lax.psum(shares[2].astype(jnp.bfloat16), "seq").astype(jnp.float32),
        lax.psum(shares[3].astype(jnp.bfloat16), "seq").astype(jnp.float32),
        lax.psum(shares[4].astype(jnp.bfloat16), "seq").astype(jnp.float32),
        lax.psum(shares[5].astype(jnp.bfloat16), "seq").astype(jnp.float32),
        lax.psum(shares[6].astype(jnp.bfloat16), "seq").astype(jnp.float32),
        lax.psum(shares[7].astype(jnp.bfloat16), "seq").astype(jnp.float32),
        lax.psum(shares[8].astype(jnp.bfloat16), "seq").astype(jnp.float32),
        lax.psum(shares[9].astype(jnp.bfloat16), "seq").astype(jnp.float32),
        lax.psum(shares[10].astype(jnp.bfloat16), "seq").astype(jnp.float32),
        lax.psum(shares[11].astype(jnp.bfloat16), "seq").astype(jnp.float32),
        lax.psum(shares[12].astype(jnp.bfloat16), "seq").astype(jnp.float32),
    )
    return (
        layer_out,
        input_grad,
        finals[0],
        finals[1],
        finals[2],
        finals[3],
        finals[4],
        finals[5],
        finals[6],
        finals[7],
        finals[8],
        finals[9],
        finals[10],
        finals[11],
        finals[12],
    )


def solution(mesh):
    in_specs = (
        P("fsdp", "seq", None),
        P("fsdp", "seq"),
        P("fsdp", None),
        P("fsdp", None),
        P("fsdp", None),
        P("fsdp", None),
        P("fsdp", None),
        P("fsdp", None),
        P("fsdp", None),
        P("fsdp"),
        P("fsdp"),
        P("fsdp"),
        P("fsdp"),
        P("fsdp"),
        P("fsdp"),
        P("fsdp", "seq", None),
    )
    out_specs = (
        P("fsdp", "seq", None),
        P("fsdp", "seq", None),
        P("fsdp", None),
        P("fsdp", None),
        P("fsdp", None),
        P("fsdp", None),
        P("fsdp", None),
        P("fsdp", None),
        P("fsdp", None),
        P("fsdp"),
        P("fsdp"),
        P("fsdp"),
        P("fsdp"),
        P("fsdp"),
        P("fsdp"),
    )
    return jax.shard_map(body, mesh=mesh, in_specs=in_specs, out_specs=out_specs, check_vma=False)
```

profile of v0, /device:TPU:0, one launch (start us, length us, event | category | flops | bytes accessed | tf_op | source)
XLA Modules:
  0.0 709.7 jit_solution(8686373132811952509)
XLA Ops:
  7.2 2.0 pad_maximum_fusion.5
  10.2 1.1 pad_maximum_fusion.2
  15.6 10.3 %all-reduce.19 = (bf16[640]{0:T(1024)(128)(2,1)S(1)}, bf16[256]{0:T(256)(128)(2,1)S(1)}, bf16[256]{0:T(256)(128)(2,1)S(1)}, bf16[640]{0:T(1024)(128)(2,1)S(1)}, ...) all-reduce(bf16[640]{0:T(1024)(128)(2,1)S(1)} %dynamic-update-slice, ...), channel_id=1, replica_groups=mesh['seq'=32,'fsdp'=4] {'fsdp'}, use_global_device_ids=true, to_apply=%add.4 | all-reduce | flops 3072 | bytes 12288
  27.7 1.5 fusion.29
  30.2 8.4 %all-gather.5.cloned.1.call-done = bf16[640,1536]{1,0:T(8,128)(2,1)} async-done(((bf16[160,1536]{1,0:T(8,128)(2,1)}), bf16[640,1536]{1,0:T(8,128)(2,1)}) %all-gather.5.cloned.1.call-update) | async-done | bytes 1966096 | tf_op jit(solution)/shard_map/all_gather | solution.py:18
  38.7 2.1 convolution_convert_fusion.8
  40.8 4.1 collective-permute-start
  44.8 1.5 multiply_reduce_fusion.12
  47.6 3.9 collective-permute-start.1
  51.6 1.4 copy.43
  53.1 2.4 multiply_reduce_fusion.2
  58.5 2.6 fusion.106
  61.1 1.2 fusion.3
  62.3 2.1 copy-done
  64.5 2.6 fusion.39
  67.1 2.8 multiply_reduce_fusion.9
  71.4 1.0 multiply_convert_fusion.2
  72.5 41.2 %all-gather.9.cloned.1.call-done = bf16[640,4096]{1,0:T(8,128)(2,1)} async-done(((bf16[160,4096]{1,0:T(8,128)(2,1)}), bf16[640,4096]{1,0:T(8,128)(2,1)}) %all-gather.9.cloned.1.call-update) | async-done | bytes 5242896 | tf_op jit(solution)/shard_map/all_gather | solution.py:18
  113.6 3.9 fusion.22
  117.5 2.0 copy-done.67
  119.5 4.5 multiply_convert_fusion.1
  124.0 20.2 %all-gather.11.cloned.1.call-done = bf16[2048,640]{1,0:T(8,128)(2,1)} async-done(((bf16[512,640]{1,0:T(8,128)(2,1)}), bf16[2048,640]{1,0:T(8,128)(2,1)}) %all-gather.11.cloned.1.call-update) | async-done | bytes 2621456 | tf_op jit(solution)/shard_map/all_gather | solution.py:97
  144.2 4.4 multiply_reduce_fusion.7
  149.2 1.4 fusion.54
  150.6 4.7 fusion.11
  155.3 1.9 fusion.16
  157.4 2.1 multiply_reduce_fusion.3
  160.7 1.4 copy-done.59
  162.2 1.0 convolution_convert_fusion.5
  163.2 2.8 fusion
  166.0 2.7 fusion.2
  168.7 1.3 fusion.43
  170.1 1.4 collective-permute-start.2
  171.5 1.3 fusion.40
  172.8 1.4 collective-permute-start.3
  174.3 7.0 collective-permute-done.2
  181.4 2.2 bitcast_multiply_fusion.1
  187.0 1.1 convolution_convert_fusion.4
  189.4 1.5 pad_maximum_fusion.1
  190.9 3.3 convolution_convert_fusion.2
  194.3 1.6 convolution_convert_fusion.1
  195.8 2.7 pad_maximum_fusion
  199.6 3.3 convolution_convert_fusion.3
  202.9 5.2 convolution_convert_fusion
  208.2 22.5 %reduce-scatter.5.cloned.1.call-done = bf16[160,1536]{1,0:T(8,128)(2,1)} async-done(((bf16[640,1536]{1,0:T(8,128)(2,1)}), bf16[160,1536]{1,0:T(8,128)(2,1)}) %reduce-scatter.5.cloned.1.call-update) | async-done | bytes 491536 | tf_op jit(solution)/shard_map/reduce_scatter | solution.py:29
  230.7 1.7 slice.62
  232.5 1.6 fusion.104
  234.1 57.1 %reduce-scatter.9.cloned.1.call-done = bf16[160,4096]{1,0:T(8,128)(2,1)} async-done(((bf16[640,4096]{1,0:T(8,128)(2,1)}), bf16[160,4096]{1,0:T(8,128)(2,1)}) %reduce-scatter.9.cloned.1.call-update) | async-done | bytes 1310736 | tf_op jit(solution)/shard_map/reduce_scatter | solution.py:29
  291.2 2.5 fusion.102
  293.7 33.6 %reduce-scatter.7.cloned.1.call-done = bf16[256,640]{1,0:T(8,128)(2,1)} async-done(((bf16[1024,640]{1,0:T(8,128)(2,1)}), bf16[256,640]{1,0:T(8,128)(2,1)}) %reduce-scatter.7.cloned.1.call-update) | async-done | bytes 327696 | tf_op jit(solution)/shard_map/reduce_scatter | solution.py:275
  327.3 43.9 %reduce-scatter.11.cloned.1.call-done = bf16[512,640]{1,0:T(8,128)(2,1)} async-done(((bf16[2048,640]{1,0:T(8,128)(2,1)}), bf16[512,640]{1,0:T(8,128)(2,1)}) %reduce-scatter.11.cloned.1.call-update) | async-done | bytes 655376 | tf_op jit(solution)/shard_map/reduce_scatter | solution.py:286
  372.5 2.2 fusion.59
  376.0 2.7 fusion.49
  378.7 7.4 %all-reduce.18 = (bf16[640]{0:T(1024)(128)(2,1)S(1)}, bf16[640]{0:T(1024)(128)(2,1)S(1)}, bf16[640]{0:T(1024)(128)(2,1)S(1)}, bf16[640]{0:T(1024)(128)(2,1)S(1)}...) all-reduce(bf16[640]{0:T(1024)(128)(2,1)S(1)} %get-tuple-element.23, ...), channel_id=6, replica_groups=mesh['seq'=32,'fsdp'=4] {'fsdp'}, use_global_device_ids=true, to_apply=%region_27.28.clone | all-reduce | flops 3072 | bytes 12288
  386.6 83.4 %all-reduce.16 = (bf16[160]{0:T(256)(128)(2,1)S(1)}, bf16[160]{0:T(256)(128)(2,1)S(1)}, bf16[160]{0:T(256)(128)(2,1)S(1)}, bf16[160]{0:T(256)(128)(2,1)S(1)}, bf...) all-reduce(bf16[160]{0:T(256)(128)(2,1)S(1)} %dynamic-slice.7, ...), channel_id=1, replica_groups=mesh['seq'=32,'fsdp'=4] {'seq'}, use_global_device_ids=true, to_apply=%region_28.29 | all-reduce | flops 768 | bytes 3072 | tf_op jit(solution)/shard_map/psum | solution.py:316
  473.3 2.7 fusion.57
  476.0 216.3 %all-reduce.22.cloned.1.call-done = (bf16[160,1024]{1,0:T(8,128)(2,1)}, bf16[160,256]{1,0:T(8,128)(2,1)}, bf16[160,256]{1,0:T(8,128)(2,1)}, bf16[256,640]{1,0:T(...) async-done(((bf16[160,1024]{1,0:T(8,128)(2,1)}, bf16[160,256]{1,0:T(8,128)(2,1)}, bf16[160,256]{1,0:T(8,128)(2,1)}, ...) | async-done | bytes 2785296 | tf_op jit(solution)/shard_map/psum | solution.py:309
  692.4 1.6 convert_element_type.268
  694.0 1.6 convert_element_type.269
  695.6 1.9 convert_element_type.267
  697.5 1.9 convert_element_type.271
  699.4 1.2 convert_element_type.274
  700.6 1.2 convert_element_type.275
  701.8 1.1 convert_element_type.277
  (248 shorter events, 25.2 us)
Async XLA Ops:
  7.2 3.0 copy-start.23
  7.2 3.0 copy-start.24
  7.2 31.5 %all-gather.5.cloned.1.call-start = ((), (), s32[]{:S(2)}) async-start(), calls=%async_computation.4 | async-start | bytes 2457600 | tf_op jit(solution)/shard_map/all_gather | solution.py:18
  9.2 57.9 %all-gather.7.cloned.1.call-start = ((), (), s32[]{:S(2)}) async-start(), calls=%async_computation.5 | async-start | bytes 1638400 | tf_op jit(solution)/shard_map/all_gather | solution.py:95
  10.0 2.0 copy-start.56
  10.0 3.9 copy-start.5
  10.0 4.2 copy-start.53
  10.0 4.2 copy-start.60
  10.0 4.4 copy-start.61
  10.0 4.7 copy-start.62
  10.1 4.9 copy-start.63
  10.1 5.1 copy-start.64
  10.1 5.3 copy-start.65
  10.1 103.5 %all-gather.9.cloned.1.call-start = ((), (), s32[]{:S(2)}) async-start(), calls=%async_computation.6 | async-start | bytes 6553600 | tf_op jit(solution)/shard_map/all_gather | solution.py:18
  11.3 132.9 %all-gather.11.cloned.1.call-start = ((), (), s32[]{:S(2)}) async-start(), calls=%async_computation.7 | async-start | bytes 3276800 | tf_op jit(solution)/shard_map/all_gather | solution.py:97
  11.9 218.8 %reduce-scatter.5.cloned.1.call-start = ((), (), s32[]{:S(2)}) async-start(), calls=%async_computation.8 | async-start | bytes 2457600 | tf_op jit(solution)/shard_map/reduce_scatter | solution.py:29
  14.1 32.3 %copy-start.47 = (f32[512]{0:T(512)}, f32[512]{0:T(512)S(1)}, u32[]{:S(2)}) copy-start(f32[512]{0:T(512)S(1)} %fusion.50) | copy-start | bytes 6148
  14.1 38.9 %copy-start.45 = (f32[512]{0:T(512)}, f32[512]{0:T(512)S(1)}, u32[]{:S(2)}) copy-start(f32[512]{0:T(512)S(1)} %fusion.84) | copy-start | bytes 6148
  26.5 20.1 %copy-start.49 = (f32[256]{0:T(256)}, f32[256]{0:T(256)S(1)}, u32[]{:S(2)}) copy-start(f32[256]{0:T(256)S(1)} %convert_element_type.231) | copy-start | bytes 3076
  26.5 26.6 %copy-start.38 = (f32[640]{0:T(1024)}, f32[640]{0:T(1024)S(1)}, u32[]{:S(2)}) copy-start(f32[640]{0:T(1024)S(1)} %convert_element_type.228) | copy-start | bytes 7684
  30.2 16.4 %copy-start.11 = (f32[512,128]{0,1:T(8,128)}, f32[512,128]{0,1:T(8,128)S(1)}, u32[]{:S(2)}) copy-start(f32[512,128]{0,1:T(8,128)S(1)} %get-tuple-element.79) | copy-start | bytes 786436
  30.2 16.4 %copy-start.13 = (f32[512,128]{0,1:T(8,128)}, f32[512,128]{0,1:T(8,128)S(1)}, u32[]{:S(2)}) copy-start(f32[512,128]{0,1:T(8,128)S(1)} %get-tuple-element.80) | copy-start | bytes 786436
  40.8 21.6 %collective-permute-start = (bf16[512,256]{1,0:T(8,128)(2,1)}, bf16[512,256]{1,0:T(8,128)(2,1)}, u32[]{:S(2)}, u32[]{:S(2)}) collective-permute-start(bf16[512,256]{1,0:T(8,128)(2,1)} %convolution_convert_fusion.8), channel_id=1, source_target_pairs={{0,4},{4,8},{8,12},{12,16},{16,20},{20,24},{24,28},{28,32},{32,36}... | collective-permute-start | bytes 786440 | tf_op jit(solution)/shard_map/ppermute | solution.py:24
  46.5 4.9 copy-start.16
  47.6 10.7 %copy-start.18 = (bf16[512,256]{0,1:T(8,128)(2,1)}, bf16[512,256]{0,1:T(8,128)(2,1)S(1)}, u32[]{:S(2)}) copy-start(bf16[512,256]{0,1:T(8,128)(2,1)S(1)} %get-tuple-element.76) | copy-start | bytes 786436
  47.6 10.6 %collective-permute-start.1 = (bf16[512,256]{0,1:T(8,128)(2,1)S(1)}, bf16[512,256]{0,1:T(8,128)(2,1)}, u32[]{:S(2)}, u32[]{:S(2)}) collective-permute-start(bf16[512,256]{0,1:T(8,128)(2,1)S(1)} %get-tuple-element.76), channel_id=1, source_target_pairs={{0,4},{4,8},{8,12},{12,16},{16,20},{20,24},{24,28},{28,32},{32,36}... | collective-permute-start | bytes 786440 | tf_op jit(solution)/shard_map/ppermute | solution.py:24
  53.1 3.1 copy-start.51
  58.2 2.9 copy-start.21
  61.1 3.3 copy-start
  61.1 3.3 copy-start.43
  67.0 2.9 copy-start.66
  67.1 3.9 copy-start.6
  113.6 5.9 copy-start.27
  113.6 5.9 copy-start.57
  144.2 4.4 copy-start.10
  144.2 4.4 copy-start.37
  144.2 6.4 copy-start.68
  144.2 6.4 copy-start.72
  149.2 6.1 slice-start.2
  150.6 4.7 copy-start.25
  150.6 4.7 slice-start.3
  155.3 2.1 copy-start.71
  155.3 7.9 %slice-start = ((s8[8388608]{0:T(1024)(128)(4,1)}), s8[4194304]{0:T(1024)(128)(4,1)S(1)}, s32[]{:S(2)}) async-start(s8[8388608]{0:T(1024)(128)(4,1)} %bitcast.145), calls=%async_computation.13 | async-start | bytes 8388608
  157.4 2.1 copy-start.2
  157.4 5.8 slice-start.1
  160.4 2.8 copy-start.3
  166.0 2.7 copy-start.22
  170.1 11.2 %copy-start.14 = (f32[512,128]{0,1:T(8,128)S(1)}, f32[512,128]{0,1:T(8,128)}, u32[]{:S(2)}) copy-start(f32[512,128]{0,1:T(8,128)} %copy-done.13) | copy-start | bytes 786436
  170.1 11.2 %collective-permute-start.2 = (bf16[512,256]{0,1:T(8,128)(2,1)S(1)}, bf16[512,256]{0,1:T(8,128)(2,1)S(1)}, u32[]{:S(2)}, u32[]{:S(2)}) collective-permute-start(bf16[512,256]{0,1:T(8,128)(2,1)S(1)} %slice.82), channel_id=1, source_target_pairs={{4,0},{8,4},{12,8},{16,12},{20,16},{24,20},{28,24},{32,28},{36,32}... | collective-permute-start | bytes 786440 | tf_op jit(solution)/shard_map/ppermute | solution.py:24
  172.8 16.0 %copy-start.34 = (f32[1024,256]{1,0:T(8,128)}, f32[1024,256]{1,0:T(8,128)S(1)}, u32[]{:S(2)}) copy-start(f32[1024,256]{1,0:T(8,128)S(1)} %fusion.40) | copy-start | bytes 3145732
  172.8 8.6 %copy-start.19 = (bf16[512,256]{0,1:T(8,128)(2,1)S(1)}, bf16[512,256]{0,1:T(8,128)(2,1)}, u32[]{:S(2)}) copy-start(bf16[512,256]{0,1:T(8,128)(2,1)} %copy-done.18) | copy-start | bytes 786436
  172.8 16.0 %collective-permute-start.3 = (bf16[512,256]{1,0:T(8,128)(2,1)S(1)}, bf16[512,256]{1,0:T(8,128)(2,1)S(1)}, u32[]{:S(2)}, u32[]{:S(2)}) collective-permute-start(bf16[512,256]{1,0:T(8,128)(2,1)S(1)} %slice.81), channel_id=1, source_target_pairs={{4,0},{8,4},{12,8},{16,12},{20,16},{24,20},{28,24},{32,28},{36,32}... | collective-permute-start | bytes 786440 | tf_op jit(solution)/shard_map/ppermute | solution.py:24
  190.9 100.3 %reduce-scatter.9.cloned.1.call-start = ((), (), s32[]{:S(2)}) async-start(), calls=%async_computation.10 | async-start | bytes 6553600 | tf_op jit(solution)/shard_map/reduce_scatter | solution.py:29
  190.9 3.3 copy-start.70
  198.5 4.4 copy-start.26
  198.5 128.7 %reduce-scatter.7.cloned.1.call-start = ((), (), s32[]{:S(2)}) async-start(), calls=%async_computation.9 | async-start | bytes 1638400 | tf_op jit(solution)/shard_map/reduce_scatter | solution.py:275
  202.9 168.3 %reduce-scatter.11.cloned.1.call-start = ((), (), s32[]{:S(2)}) async-start(), calls=%async_computation.11 | async-start | bytes 3276800 | tf_op jit(solution)/shard_map/reduce_scatter | solution.py:286
  208.2 484.2 %all-reduce.22.cloned.1.call-start = ((), (), s32[]{:S(2)}) async-start(), calls=%async_computation.12 | async-start | bytes 5570560 | tf_op jit(solution)/shard_map/psum | solution.py:309
  234.1 138.5 %copy-start.17 = (bf16[640,1536]{1,0:T(8,128)(2,1)S(1)}, bf16[640,1536]{1,0:T(8,128)(2,1)}, u32[]{:S(2)}) copy-start(bf16[640,1536]{1,0:T(8,128)(2,1)} %all-gather.5.cloned.1.call-done) | copy-start | bytes 5898244
  376.0 97.3 %copy-start.48 = (f32[512]{0:T(512)S(1)}, f32[512]{0:T(512)}, u32[]{:S(2)}) copy-start(f32[512]{0:T(512)} %copy-done.47) | copy-start | bytes 6148
  376.0 97.3 %copy-start.4 = (f32[512,640]{1,0:T(8,128)S(1)}, f32[512,640]{1,0:T(8,128)}, u32[]{:S(2)}) copy-start(f32[512,640]{1,0:T(8,128)} %copy-done.3) | copy-start | bytes 3932164
  692.4 7.0 copy-start.33
  694.0 6.6 copy-start.32
  699.4 2.4 copy-start.31
  (26 other events, 32.8 us)
Sparse Core Ops, SparseCore 0:
  10.3 28.3 all-gather.4
  40.3 21.7 all-gather.6
  64.4 49.1 all-gather.8
  115.1 29.0 all-gather.10
  191.0 39.6 reduce-scatter.4
  233.4 57.7 reduce-scatter.8
  294.4 32.8 reduce-scatter.6
  330.1 41.0 reduce-scatter.10
  374.8 317.4 all-reduce.21
where the time goes:
time: 715 us; the launch traced here: 710 us
  waiting for transfers between devices  452 us (63%)
  blocking collectives  101 us (14%)
  matrix products  64.8 us (9%)
  other arithmetic  41.5 us (6%)
  local copies, waits for them, and re-layouts  21.3 us (3%)
  between operations  17.9 us (3%)
  starting transfers between devices  11.4 us (2%)
    psum x1, waiting for transfers between devices, body(): lax.psum(shares[0].astype(jnp.bfloat16), 'seq').astype(jnp.float32)  216 us
    psum x1, blocking collectives, body(): lax.psum(shares[7].astype(jnp.bfloat16), 'seq').astype(jnp.float32)  83.4 us
    reduce_scatter x2, waiting for transfers between devices, side_by_side_2(): lax.psum_scatter(both, axis, scatter_dimension=dim, tiled=True)  79.6 us
    all_gather x2, waiting for transfers between devices, side_by_side(): lax.all_gather(both, axis, axis=dim, tiled=True)  49.6 us
    reduce_scatter x1, waiting for transfers between devices, body(): lax.psum_scatter(grad_down.astype(jnp.bfloat16), 'fsdp', scatter_dimensio...  43.9 us
    reduce_scatter x1, waiting for transfers between devices, body(): lax.psum_scatter(grad_output.astype(jnp.bfloat16), 'fsdp', scatter_dimens...  33.6 us
    dot_general x7, matrix products, forward_dot(): return jnp.dot(left, right, preferred_element_type=jnp.float32)  21.6 us
    all_gather x1, waiting for transfers between devices, body(): lax.all_gather(w_down, 'fsdp', axis=0, tiled=True)  20.2 us
  transfers between devices with their start and end apart: 13, of which 9 were waited for; matrix products, arithmetic and copies ran while one was open for 11% of the time, Pallas kernels for 0%

commit v1 on v0

--- a/solution.py
+++ b/solution.py
@@ -306,7 +306,7 @@
         ).astype(jnp.float32),
     )
     finals = (
-        lax.psum(shares[0].astype(jnp.bfloat16), "seq").astype(jnp.float32),
+        jnp.sum(lax.all_gather(shares[0].astype(jnp.bfloat16), "seq"), axis=0).astype(jnp.float32),
         lax.psum(shares[1].astype(jnp.bfloat16), "seq").astype(jnp.float32),
         lax.psum(shares[2].astype(jnp.bfloat16), "seq").astype(jnp.float32),
         lax.psum(shares[3].astype(jnp.bfloat16), "seq").astype(jnp.float32),

time: 715 us -> 879 us (1.23)
  waiting for transfers between devices: 452 us -> 608 us
    all_gather x0 -> x1, waiting for transfers between devices: none -> 161 us  [body(): lax.all_gather(shares[0].astype(jnp.bfloat16), 'seq')]
  transfers between devices with their start and end apart: 13 -> 14, of which waited for: 9 -> 10; matrix products, arithmetic and copies ran while one was open for 11% -> 10% of each run, Pallas kernels for 0% -> 0%
where the time goes in v1:
time: 879 us; the launch traced here: 874 us
  waiting for transfers between devices  608 us (69%)
  blocking collectives  101 us (11%)
  matrix products  65.5 us (7%)
  other arithmetic  49 us (6%)
  local copies, waits for them, and re-layouts  20.6 us (2%)
  between operations  18.2 us (2%)
  starting transfers between devices  11 us (1%)
    psum x1, waiting for transfers between devices, body(): lax.psum(shares[1].astype(jnp.bfloat16), 'seq').astype(jnp.float32)  210 us
    all_gather x1, waiting for transfers between devices, body(): lax.all_gather(shares[0].astype(jnp.bfloat16), 'seq')  161 us
    psum x1, blocking collectives, body(): lax.psum(shares[7].astype(jnp.bfloat16), 'seq').astype(jnp.float32)  83.4 us
    reduce_scatter x2, waiting for transfers between devices, side_by_side_2(): lax.psum_scatter(both, axis, scatter_dimension=dim, tiled=True)  81.4 us
    all_gather x2, waiting for transfers between devices, side_by_side(): lax.all_gather(both, axis, axis=dim, tiled=True)  50 us
    reduce_scatter x1, waiting for transfers between devices, body(): lax.psum_scatter(grad_down.astype(jnp.bfloat16), 'fsdp', scatter_dimensio...  43.9 us
    reduce_scatter x1, waiting for transfers between devices, body(): lax.psum_scatter(grad_output.astype(jnp.bfloat16), 'fsdp', scatter_dimens...  33.6 us
    dot_general x7, matrix products, forward_dot(): return jnp.dot(left, right, preferred_element_type=jnp.float32)  21.6 us
  transfers between devices with their start and end apart: 14, of which 10 were waited for; matrix products, arithmetic and copies ran while one was open for 10% of the time, Pallas kernels for 0%

profile of v1, /device:TPU:0, one launch (start us, length us, event | category | flops | bytes accessed | tf_op | source)
XLA Modules:
  0.0 873.8 jit_solution(8255931573292414710)
XLA Ops:
  7.2 2.0 pad_maximum_fusion.5
  10.2 1.1 pad_maximum_fusion.2
  15.6 10.3 %all-reduce.19 = (bf16[640]{0:T(1024)(128)(2,1)S(1)}, bf16[256]{0:T(256)(128)(2,1)S(1)}, bf16[256]{0:T(256)(128)(2,1)S(1)}, bf16[640]{0:T(1024)(128)(2,1)S(1)}, ...) all-reduce(bf16[640]{0:T(1024)(128)(2,1)S(1)} %dynamic-update-slice, ...), channel_id=1, replica_groups=mesh['seq'=32,'fsdp'=4] {'fsdp'}, use_global_device_ids=true, to_apply=%add.4 | all-reduce | flops 3072 | bytes 12288
  27.7 1.5 fusion.29
  30.2 8.4 all-gather.7.cloned.1.call-done
  38.7 2.1 convolution_convert_fusion.8
  40.8 4.1 collective-permute-start
  44.8 1.5 multiply_reduce_fusion.12
  47.6 3.5 collective-permute-start.1
  51.3 1.4 copy.43
  52.7 2.4 multiply_reduce_fusion.2
  58.1 2.6 fusion.106
  60.8 1.2 fusion.3
  62.0 2.1 copy-done
  64.1 2.6 fusion.39
  66.7 2.8 multiply_reduce_fusion.9
  71.1 1.0 multiply_convert_fusion.2
  72.1 41.5 %all-gather.11.cloned.1.call-done = bf16[640,4096]{1,0:T(8,128)(2,1)} async-done(((bf16[160,4096]{1,0:T(8,128)(2,1)}), bf16[640,4096]{1,0:T(8,128)(2,1)}) %all-gather.11.cloned.1.call-update) | async-done | bytes 5242896 | tf_op jit(solution)/shard_map/all_gather | solution.py:18
  113.6 3.9 fusion.22
  117.5 2.0 copy-done.71
  119.5 4.5 multiply_convert_fusion.1
  124.0 20.2 %all-gather.13.cloned.1.call-done = bf16[2048,640]{1,0:T(8,128)(2,1)} async-done(((bf16[512,640]{1,0:T(8,128)(2,1)}), bf16[2048,640]{1,0:T(8,128)(2,1)}) %all-gather.13.cloned.1.call-update) | async-done | bytes 2621456 | tf_op jit(solution)/shard_map/all_gather | solution.py:97
  144.2 4.4 multiply_reduce_fusion.7
  149.2 1.4 fusion.54
  150.6 4.7 fusion.11
  155.3 1.9 fusion.16
  157.4 2.6 multiply_reduce_fusion.3
  161.3 1.4 copy-done.63
  163.8 2.8 fusion
  166.6 2.9 fusion.2
  169.5 1.3 fusion.43
  170.8 1.4 collective-permute-start.2
  172.2 1.3 fusion.40
  173.6 1.4 collective-permute-start.3
  175.0 7.0 collective-permute-done.2
  182.1 2.3 bitcast_multiply_fusion.1
  185.8 1.4 multiply_reduce_fusion
  188.4 1.1 convolution_convert_fusion.4
  190.9 1.5 pad_maximum_fusion.1
  192.4 3.3 convolution_convert_fusion.2
  195.8 1.6 convolution_convert_fusion.1
  197.3 2.7 pad_maximum_fusion
  201.1 3.3 convolution_convert_fusion.3
  204.5 5.2 convolution_convert_fusion
  209.7 22.5 %reduce-scatter.5.cloned.1.call-done = bf16[160,1536]{1,0:T(8,128)(2,1)} async-done(((bf16[640,1536]{1,0:T(8,128)(2,1)}), bf16[160,1536]{1,0:T(8,128)(2,1)}) %reduce-scatter.5.cloned.1.call-update) | async-done | bytes 491536 | tf_op jit(solution)/shard_map/reduce_scatter | solution.py:29
  232.2 1.6 fusion.104
  233.8 58.8 %reduce-scatter.9.cloned.1.call-done = bf16[160,4096]{1,0:T(8,128)(2,1)} async-done(((bf16[640,4096]{1,0:T(8,128)(2,1)}), bf16[160,4096]{1,0:T(8,128)(2,1)}) %reduce-scatter.9.cloned.1.call-update) | async-done | bytes 1310736 | tf_op jit(solution)/shard_map/reduce_scatter | solution.py:29
  292.7 2.5 fusion.102
  295.2 33.6 %reduce-scatter.7.cloned.1.call-done = bf16[256,640]{1,0:T(8,128)(2,1)} async-done(((bf16[1024,640]{1,0:T(8,128)(2,1)}), bf16[256,640]{1,0:T(8,128)(2,1)}) %reduce-scatter.7.cloned.1.call-update) | async-done | bytes 327696 | tf_op jit(solution)/shard_map/reduce_scatter | solution.py:275
  328.8 43.9 %reduce-scatter.11.cloned.1.call-done = bf16[512,640]{1,0:T(8,128)(2,1)} async-done(((bf16[2048,640]{1,0:T(8,128)(2,1)}), bf16[512,640]{1,0:T(8,128)(2,1)}) %reduce-scatter.11.cloned.1.call-update) | async-done | bytes 655376 | tf_op jit(solution)/shard_map/reduce_scatter | solution.py:286
  374.9 2.2 fusion.59
  378.4 2.7 fusion.49
  381.1 7.5 all-reduce.18
  389.0 83.4 %all-reduce.16 = (bf16[160]{0:T(256)(128)(2,1)S(1)}, bf16[160]{0:T(256)(128)(2,1)S(1)}, bf16[160]{0:T(256)(128)(2,1)S(1)}, bf16[160]{0:T(256)(128)(2,1)S(1)}, bf...) all-reduce(bf16[160]{0:T(256)(128)(2,1)S(1)} %dynamic-slice.7, ...), channel_id=1, replica_groups=mesh['seq'=32,'fsdp'=4] {'seq'}, use_global_device_ids=true, to_apply=%region_28.29 | all-reduce | flops 768 | bytes 3072 | tf_op jit(solution)/shard_map/psum | solution.py:316
  475.7 2.7 fusion.57
  478.5 210.0 %all-reduce.22.cloned.1.call-done = (bf16[160,256]{1,0:T(8,128)(2,1)}, bf16[160,256]{1,0:T(8,128)(2,1)}, bf16[256,640]{1,0:T(8,128)(2,1)}, bf16[160,2048]{1,0:T(...) async-done(((bf16[160,256]{1,0:T(8,128)(2,1)}, bf16[160,256]{1,0:T(8,128)(2,1)}, bf16[256,640]{1,0:T(8,128)(2,1)}, bf16[160,2048]{1,0:T(8,128)(2,1)}, ...) | async-done | bytes 2457616 | tf_op jit(solution)/shard_map/psum | solution.py:310
  688.5 1.6 convert_element_type.270
  690.1 1.6 convert_element_type.271
  691.7 1.9 convert_element_type.273
  693.5 2.4 convert_element_type.276
  695.9 1.2 convert_element_type.277
  697.1 1.1 convert_element_type.279
  698.2 160.9 %all-gather.15.cloned.1.call-done = bf16[5120,1024]{1,0:T(8,128)(2,1)} async-done(((bf16[160,1024]{1,0:T(8,128)(2,1)}), bf16[5120,1024]{1,0:T(8,128)(2,1)}) %all-gather.15.cloned.1.call-update) | async-done | bytes 10485776 | tf_op jit(solution)/shard_map/all_gather | solution.py:309
  859.1 6.7 reduce_sum.212
  (260 shorter events, 27.3 us)
Async XLA Ops:
  7.2 3.0 copy-start.23
  7.2 3.0 copy-start.24
  7.2 31.5 %all-gather.7.cloned.1.call-start = ((), (), s32[]{:S(2)}) async-start(), calls=%async_computation.4 | async-start | bytes 2457600 | tf_op jit(solution)/shard_map/all_gather | solution.py:18
  9.2 57.5 %all-gather.9.cloned.1.call-start = ((), (), s32[]{:S(2)}) async-start(), calls=%async_computation.5 | async-start | bytes 1638400 | tf_op jit(solution)/shard_map/all_gather | solution.py:95
  10.0 3.9 copy-start.5
  10.0 4.2 copy-start.55
  10.0 4.2 copy-start.64
  10.0 4.4 copy-start.65
  10.0 4.7 copy-start.66
  10.1 4.9 copy-start.67
  10.1 5.1 copy-start.68
  10.1 5.3 copy-start.69
  10.1 103.5 %all-gather.11.cloned.1.call-start = ((), (), s32[]{:S(2)}) async-start(), calls=%async_computation.6 | async-start | bytes 6553600 | tf_op jit(solution)/shard_map/all_gather | solution.py:18
  11.3 132.9 %all-gather.13.cloned.1.call-start = ((), (), s32[]{:S(2)}) async-start(), calls=%async_computation.7 | async-start | bytes 3276800 | tf_op jit(solution)/shard_map/all_gather | solution.py:97
  11.9 220.3 %reduce-scatter.5.cloned.1.call-start = ((), (), s32[]{:S(2)}) async-start(), calls=%async_computation.8 | async-start | bytes 2457600 | tf_op jit(solution)/shard_map/reduce_scatter | solution.py:29
  14.1 32.2 %copy-start.49 = (f32[512]{0:T(512)}, f32[512]{0:T(512)S(1)}, u32[]{:S(2)}) copy-start(f32[512]{0:T(512)S(1)} %fusion.50) | copy-start | bytes 6148
  14.1 38.6 %copy-start.47 = (f32[512]{0:T(512)}, f32[512]{0:T(512)S(1)}, u32[]{:S(2)}) copy-start(f32[512]{0:T(512)S(1)} %fusion.84) | copy-start | bytes 6148
  26.5 20.0 %copy-start.51 = (f32[256]{0:T(256)}, f32[256]{0:T(256)S(1)}, u32[]{:S(2)}) copy-start(f32[256]{0:T(256)S(1)} %convert_element_type.233) | copy-start | bytes 3076
  26.5 26.2 %copy-start.40 = (f32[640]{0:T(1024)}, f32[640]{0:T(1024)S(1)}, u32[]{:S(2)}) copy-start(f32[640]{0:T(1024)S(1)} %convert_element_type.230) | copy-start | bytes 7684
  30.2 16.4 %copy-start.11 = (f32[512,128]{0,1:T(8,128)}, f32[512,128]{0,1:T(8,128)S(1)}, u32[]{:S(2)}) copy-start(f32[512,128]{0,1:T(8,128)S(1)} %get-tuple-element.78) | copy-start | bytes 786436
  30.2 16.4 %copy-start.13 = (f32[512,128]{0,1:T(8,128)}, f32[512,128]{0,1:T(8,128)S(1)}, u32[]{:S(2)}) copy-start(f32[512,128]{0,1:T(8,128)S(1)} %get-tuple-element.79) | copy-start | bytes 786436
  40.8 21.2 %collective-permute-start = (bf16[512,256]{1,0:T(8,128)(2,1)}, bf16[512,256]{1,0:T(8,128)(2,1)}, u32[]{:S(2)}, u32[]{:S(2)}) collective-permute-start(bf16[512,256]{1,0:T(8,128)(2,1)} %convolution_convert_fusion.8), channel_id=1, source_target_pairs={{0,4},{4,8},{8,12},{12,16},{16,20},{20,24},{24,28},{28,32},{32,36}... | collective-permute-start | bytes 786440 | tf_op jit(solution)/shard_map/ppermute | solution.py:24
  46.5 4.6 copy-start.16
  47.6 10.3 %copy-start.18 = (bf16[512,256]{0,1:T(8,128)(2,1)}, bf16[512,256]{0,1:T(8,128)(2,1)S(1)}, u32[]{:S(2)}) copy-start(bf16[512,256]{0,1:T(8,128)(2,1)S(1)} %get-tuple-element.75) | copy-start | bytes 786436
  47.6 10.3 %collective-permute-start.1 = (bf16[512,256]{0,1:T(8,128)(2,1)S(1)}, bf16[512,256]{0,1:T(8,128)(2,1)}, u32[]{:S(2)}, u32[]{:S(2)}) collective-permute-start(bf16[512,256]{0,1:T(8,128)(2,1)S(1)} %get-tuple-element.75), channel_id=1, source_target_pairs={{0,4},{4,8},{8,12},{12,16},{16,20},{20,24},{24,28},{28,32},{32,36}... | collective-permute-start | bytes 786440 | tf_op jit(solution)/shard_map/ppermute | solution.py:24
  52.7 3.1 copy-start.53
  57.8 2.9 copy-start.21
  60.7 3.3 copy-start
  60.8 3.3 copy-start.45
  66.7 2.9 copy-start.70
  66.7 3.9 copy-start.6
  113.6 5.9 copy-start.27
  113.6 5.9 copy-start.61
  144.2 4.4 copy-start.10
  144.2 4.4 copy-start.39
  144.2 6.4 copy-start.72
  144.2 6.4 copy-start.76
  149.2 6.1 slice-start.2
  150.6 4.7 copy-start.25
  150.6 4.7 slice-start.3
  155.3 8.4 slice-start
  157.4 6.4 slice-start.1
  160.9 2.8 copy-start.3
  166.6 2.9 copy-start.22
  170.8 11.2 %copy-start.14 = (f32[512,128]{0,1:T(8,128)S(1)}, f32[512,128]{0,1:T(8,128)}, u32[]{:S(2)}) copy-start(f32[512,128]{0,1:T(8,128)} %copy-done.13) | copy-start | bytes 786436
  170.8 11.2 %collective-permute-start.2 = (bf16[512,256]{0,1:T(8,128)(2,1)S(1)}, bf16[512,256]{0,1:T(8,128)(2,1)S(1)}, u32[]{:S(2)}, u32[]{:S(2)}) collective-permute-start(bf16[512,256]{0,1:T(8,128)(2,1)S(1)} %slice.82), channel_id=1, source_target_pairs={{4,0},{8,4},{12,8},{16,12},{20,16},{24,20},{28,24},{32,28},{36,32}... | collective-permute-start | bytes 786440 | tf_op jit(solution)/shard_map/ppermute | solution.py:24
  173.5 16.6 %copy-start.33 = (f32[1024,256]{1,0:T(8,128)}, f32[1024,256]{1,0:T(8,128)S(1)}, u32[]{:S(2)}) copy-start(f32[1024,256]{1,0:T(8,128)S(1)} %fusion.40) | copy-start | bytes 3145732
  173.5 8.6 copy-start.19
  173.6 16.6 %collective-permute-start.3 = (bf16[512,256]{1,0:T(8,128)(2,1)S(1)}, bf16[512,256]{1,0:T(8,128)(2,1)S(1)}, u32[]{:S(2)}, u32[]{:S(2)}) collective-permute-start(bf16[512,256]{1,0:T(8,128)(2,1)S(1)} %slice.81), channel_id=1, source_target_pairs={{4,0},{8,4},{12,8},{16,12},{20,16},{24,20},{28,24},{32,28},{36,32}... | collective-permute-start | bytes 786440 | tf_op jit(solution)/shard_map/ppermute | solution.py:24
  192.4 100.3 %reduce-scatter.9.cloned.1.call-start = ((), (), s32[]{:S(2)}) async-start(), calls=%async_computation.10 | async-start | bytes 6553600 | tf_op jit(solution)/shard_map/reduce_scatter | solution.py:29
  192.4 3.3 copy-start.74
  200.1 4.4 copy-start.26
  200.1 128.7 %reduce-scatter.7.cloned.1.call-start = ((), (), s32[]{:S(2)}) async-start(), calls=%async_computation.9 | async-start | bytes 1638400 | tf_op jit(solution)/shard_map/reduce_scatter | solution.py:275
  204.4 168.3 %reduce-scatter.11.cloned.1.call-start = ((), (), s32[]{:S(2)}) async-start(), calls=%async_computation.11 | async-start | bytes 3276800 | tf_op jit(solution)/shard_map/reduce_scatter | solution.py:286
  209.7 478.8 %all-reduce.22.cloned.1.call-start = ((), (), s32[]{:S(2)}) async-start(), calls=%async_computation.13 | async-start | bytes 4915200 | tf_op jit(solution)/shard_map/psum | solution.py:310
  233.8 138.9 %copy-start.36 = (bf16[160,1536]{1,0:T(8,128)(2,1)S(1)}, bf16[160,1536]{1,0:T(8,128)(2,1)}, u32[]{:S(2)}) copy-start(bf16[160,1536]{1,0:T(8,128)(2,1)} %reduce-scatter.5.cloned.1.call-done) | copy-start | bytes 1474564
  295.2 79.7 %copy-start.17 = (bf16[640,1536]{1,0:T(8,128)(2,1)S(1)}, bf16[640,1536]{1,0:T(8,128)(2,1)}, u32[]{:S(2)}) copy-start(bf16[640,1536]{1,0:T(8,128)(2,1)} %all-gather.7.cloned.1.call-done) | copy-start | bytes 5898244
  372.7 486.4 %all-gather.15.cloned.1.call-start = ((), (), s32[]{:S(2)}) async-start(), calls=%async_computation.12 | async-start | bytes 10813440 | tf_op jit(solution)/shard_map/all_gather | solution.py:309
  378.4 2.7 copy-start.58
  378.4 2.7 copy-start.60
  378.4 97.3 %copy-start.50 = (f32[512]{0:T(512)S(1)}, f32[512]{0:T(512)}, u32[]{:S(2)}) copy-start(f32[512]{0:T(512)} %copy-done.49) | copy-start | bytes 6148
  378.4 97.3 %copy-start.4 = (f32[512,640]{1,0:T(8,128)S(1)}, f32[512,640]{1,0:T(8,128)}, u32[]{:S(2)}) copy-start(f32[512,640]{1,0:T(8,128)} %copy-done.3) | copy-start | bytes 3932164
  688.5 7.4 copy-start.32
  693.5 3.6 copy-start.31
  (31 other events, 42.6 us)
Sparse Core Ops, SparseCore 0:
  10.3 28.3 all-gather.6
  40.3 21.7 all-gather.8
  64.4 49.1 all-gather.10
  115.1 29.0 all-gather.12
  192.5 39.7 reduce-scatter.4
  234.9 57.7 reduce-scatter.8
  295.9 32.8 reduce-scatter.6
  331.6 41.0 reduce-scatter.10
  376.3 312.1 all-reduce.21
  690.0 169.0 all-gather.14
